TPU v7x, 1024 devices: a whole 4x4x32 slice. The times are simulated.
1024 devices in a mesh: dp: 16 (over x, y), fsdp: 64 (over z, core).
Axes of the slice: x: 4, y: 4, z: 32, core: 2. Of those that a mesh axis runs over, the one named last changes fastest.
Arguments:
- grads: bfloat16 [16, 128, 512, 512], P('dp', None, 'fsdp'), may hold values from -4 to 4
- left_stats: float32 [64, 4, 512, 512], P('fsdp', None, 'dp'), may hold values from -0.5 to 9, as said below
- right_stats: float32 [64, 4, 512, 512], P('fsdp', None, 'dp'), may hold values from -0.5 to 9, as said below
- left_root: bfloat16 [64, 4, 512, 512], P('fsdp', None, 'dp'), may hold values from -0.5 to 14, as said below
- right_root: bfloat16 [64, 4, 512, 512], P('fsdp'), may hold values from -0.5 to 14, as said below
- second_moment: float32 [64, 4, 512, 512], P('fsdp', None, 'dp'), may hold values from 0.2 to 2
- slot_block: int32 [64, 4], replicated, may hold values from 0 to 127, as said below
- counts: int32 [64], replicated, may hold values from 0 to 4, as said below
Outputs:
- left_new: float32 [64, 4, 512, 512], P('fsdp', None, 'dp')
- right_new: float32 [64, 4, 512, 512], P('fsdp', None, 'dp')
- second_new: float32 [64, 4, 512, 512], P('fsdp', None, 'dp')
- update: float32 [64, 4, 512, 512], P('fsdp', None, 'dp')
Inputs may be any that keep to these rules, and one draw needn't show every extreme that they name: Every owner holds counts[o] blocks; the counts sum to 128, and some owner holds exactly 4. `slot_block`: the first counts[o] slots of owner o name distinct blocks, every block is named by exactly one such slot, and later slots name arbitrary blocks. `left_stats`: Symmetric. `right_stats`: Symmetric. `left_root`: Symmetric. `right_root`: Symmetric.
All inputs are finite; a program needn't handle non-finite values.
Results may differ from a plain program's by a relative error of at most 0.015.
Values may be sent and summed in bfloat16 or wider, within the bound.
A program may use at most 32 MiB of HBM per device.

v0:
```python
import jax
import jax.numpy as jnp
from jax import lax
from jax.sharding import PartitionSpec as P

SHAMPOO_BETA = 0.998
ADAM_BETA = 0.95
EPSILON = 1e-08


def cut_along(array, dim, count):
    lengths = array.shape
    tiles = array.reshape(*lengths[:dim], count, lengths[dim] // count, *lengths[dim + 1 :])
    return jnp.moveaxis(tiles, dim, 0)


def sum_at_owner(array, axis, dim):
    tiles = cut_along(array, dim, lax.axis_size(axis))
    arrived = lax.all_to_all(tiles, axis, split_axis=0, concat_axis=0, tiled=True)
    return arrived.astype(jnp.float32).sum(axis=0)


def joined_along(tiles, dim):
    lengths = list(tiles.shape[1:])
    lengths[dim] *= tiles.shape[0]
    return jnp.moveaxis(tiles, 0, dim).reshape(lengths)


def sent_to_all(array, axis):
    copies = jnp.broadcast_to(array, (lax.axis_size(axis), *array.shape))
    return lax.all_to_all(copies, axis, split_axis=0, concat_axis=0, tiled=True)


def collect(array, axis, dim):
    return joined_along(sent_to_all(array, axis), dim)


def over_copies(array, axis):
    return sent_to_all(array, axis).sum(axis=0)


def in_one(arrays, axis):
    ends = [0]
    for a in arrays:
        ends.append(ends[-1] + a.size)
    so_far = over_copies(jnp.concatenate([a.ravel() for a in arrays]), axis)
    return tuple((so_far[b:e].reshape(a.shape) for a, b, e in zip(arrays, ends, ends[1:])))


def on_device(
    grads, left_stats, right_stats, left_root, right_root, second_moment, slot_block, counts
):
    slot_count = slot_block.shape[1]
    owner_count = slot_block.shape[0]
    block_order = left_root.shape[3]
    partial_value = grads[0]
    block_count = partial_value.shape[0]
    slab_rows = partial_value.shape[1]
    flat_slots = slot_block.reshape(-1)
    live_slots = (jnp.arange(slot_count, dtype=jnp.int32)[None, :] < counts[:, None]).reshape(-1)
    flat_partial = partial_value.reshape(block_count, slab_rows * block_order).astype(jnp.float32)
    summed = sum_at_owner(flat_partial.astype(jnp.bfloat16), "dp", 1)
    column_slab = summed.astype(jnp.bfloat16)
    picked = jnp.where(live_slots[:, None], column_slab[flat_slots], jnp.zeros((), jnp.bfloat16))
    received = lax.all_to_all(picked, "fsdp", split_axis=0, concat_axis=1, tiled=True)
    piece_width = column_slab.shape[1]
    received = received.reshape(slot_count, owner_count, piece_width)
    gathered = collect(received, "dp", 2)
    grad_full = gathered.reshape(slot_count, block_order, block_order)
    slab_width = block_order // lax.axis_size("dp")
    row_start = lax.axis_index("dp") * slab_width
    row_grad = lax.dynamic_slice_in_dim(grad_full, row_start, slab_width, 1)
    column_grad = lax.dynamic_slice_in_dim(grad_full, row_start, slab_width, 2)
    owned_here = jnp.arange(slot_count, dtype=jnp.int32) < counts[lax.axis_index("fsdp")]
    keep_mask = owned_here[:, None, None]
    left_term = jnp.einsum("crk,cjk->crj", row_grad, grad_full, preferred_element_type=jnp.float32)
    right_term = jnp.einsum(
        "ckr,ckj->crj", column_grad, grad_full, preferred_element_type=jnp.float32
    )
    left_old = left_stats[0]
    right_old = right_stats[0]
    left_new = jnp.where(
        keep_mask, SHAMPOO_BETA * left_old + (1.0 - SHAMPOO_BETA) * left_term, left_old
    )
    right_new = jnp.where(
        keep_mask, SHAMPOO_BETA * right_old + (1.0 - SHAMPOO_BETA) * right_term, right_old
    )
    left_half = jnp.einsum(
        "crk,ckj->crj", left_root[0], grad_full, preferred_element_type=jnp.float32
    ).astype(jnp.bfloat16)
    precond = jnp.einsum(
        "crk,ckj->crj", left_half, right_root[0], preferred_element_type=jnp.float32
    )
    row_values = row_grad.astype(jnp.float32)
    moment_old = second_moment[0]
    second_new = jnp.where(
        keep_mask, ADAM_BETA * moment_old + (1.0 - ADAM_BETA) * row_values * row_values, moment_old
    )
    adam = row_values / (jnp.sqrt(second_new) + EPSILON)
    precond_sum, adam_sum = in_one(
        (jnp.sum(precond * precond, axis=(1, 2)), jnp.sum(adam * adam, axis=(1, 2))), "dp"
    )
    graft_scale = jnp.where(
        owned_here, jnp.sqrt(adam_sum / jnp.where(owned_here, precond_sum, 1.0)), 0.0
    )
    update = precond * graft_scale[:, None, None]
    return (left_new[None], right_new[None], second_new[None], update[None])


def solution(mesh):
    in_specs = (
        P("dp", None, "fsdp", None),
        P("fsdp", None, "dp", None),
        P("fsdp", None, "dp", None),
        P("fsdp", None, "dp", None),
        P("fsdp", None, None, None),
        P("fsdp", None, "dp", None),
        P(),
        P(),
    )
    out_specs = (
        P("fsdp", None, "dp", None),
        P("fsdp", None, "dp", None),
        P("fsdp", None, "dp", None),
        P("fsdp", None, "dp", None),
    )
    return jax.shard_map(
        on_device, mesh=mesh, in_specs=in_specs, out_specs=out_specs, check_vma=False
    )
```

profile of v0, /device:TPU:1, one launch (start us, length us, event | category | flops | bytes accessed | tf_op | source)
XLA Modules:
  0.0 153.1 jit_solution(1414096651034471369)
XLA Ops:
  0.6 0.0 copy-start
  0.6 2.1 %copy.33 = bf16[1,128,8,512]{1,3,2,0:T(8,128)(2,1)S(1)} copy(bf16[1,128,8,512]{3,2,1,0:T(8,128)(2,1)} %param.8) | data formatting | bytes 2097152 | tf_op args[0]
  2.7 0.0 copy-start.5
  2.8 0.0 copy-start.6
  2.8 1.3 copy.34
  4.1 7.6 %all-to-all-start = ((bf16[16,128,256]{2,1,0:T(8,128)(2,1)}), bf16[16,128,256]{2,1,0:T(8,128)(2,1)S(1)}, u32[]{:S(2)}, u32[]{:S(2)}) async-start(bf16[16,128,256]{2,1,0:T(8,128)(2,1)} %copy.34), calls=%async_computation | async-start | bytes 2097152 | tf_op jit(solution)/shard_map/all_to_all | solution.py:19
  11.7 0.0 copy-done.5
  11.7 0.1 copy.35
  11.8 0.1 reshape.76
  11.9 0.1 iota_compare_fusion
  12.0 11.4 %all-to-all-done = bf16[16,128,256]{2,1,0:T(8,128)(2,1)S(1)} async-done(((bf16[16,128,256]{2,1,0:T(8,128)(2,1)}), bf16[16,128,256]{2,1,0:T(8,128)(2,1)S(1)}, u32[]{:S(2)}, u32[]{:S(2)}) %all-to-all-start) | async-done | bytes 1048608 | tf_op jit(solution)/shard_map/all_to_all | solution.py:19
  23.4 0.1 reduce_sum.39
  23.6 1.2 gather_fusion
  24.7 0.1 broadcast_select_fusion
  24.9 66.3 %all_to_all.29 = bf16[64,4,256]{2,1,0:T(4,128)(2,1)S(1)} all-to-all(bf16[64,4,256]{2,1,0:T(4,128)(2,1)S(1)} %broadcast_select_fusion), channel_id=1, replica_groups=mesh['dp'=16,'fsdp'=64] {'fsdp'}, dimensions={0} | all-to-all | bytes 262144 | tf_op jit(solution)/shard_map/all_to_all | solution.py:65
  91.2 1.6 %broadcast_in_dim.59 = bf16[16,4,64,256]{3,2,1,0:T(8,128)(2,1)} broadcast(bf16[4,64,256]{2,1,0:T(8,128)(2,1)S(1)} %copy.36), dimensions={1,2,3} | broadcast | bytes 2228224 | tf_op jit(solution)/shard_map/broadcast_in_dim | solution.py:30
  92.8 4.4 %all-to-all-start.2 = ((bf16[16,4,64,256]{3,2,1,0:T(8,128)(2,1)}), bf16[16,4,64,256]{3,2,1,0:T(8,128)(2,1)}, u32[]{:S(2)}, u32[]{:S(2)}) async-start(bf16[16,4,64,256]{3,2,1,0:T(8,128)(2,1)} %broadcast_in_dim.59), calls=%async_computation.2 | async-start | bytes 4194304 | tf_op jit(solution)/shard_map/all_to_all | solution.py:31
  97.2 0.6 dynamic_slice.9
  97.8 0.6 iota_compare_fusion.1
  98.4 24.8 %all-to-all-done.2 = bf16[16,4,64,256]{3,2,1,0:T(8,128)(2,1)} async-done(((bf16[16,4,64,256]{3,2,1,0:T(8,128)(2,1)}), bf16[16,4,64,256]{3,2,1,0:T(8,128)(2,1)}, u32[]{:S(2)}, u32[]{:S(2)}) %all-to-all-start.2) | async-done | bytes 2097184 | tf_op jit(solution)/shard_map/all_to_all | solution.py:31
  123.2 4.1 %copy.37 = bf16[4,64,16,256]{3,2,1,0:T(8,128)(2,1)} copy(bf16[4,64,16,256]{3,1,0,2:T(8,128)(2,1)} %bitcast.6) | data formatting | bytes 4194304 | tf_op jit(solution)/shard_map/transpose | solution.py:26
  127.3 4.1 %reshape_reshape.3 = bf16[4,512,512]{2,1,0:T(8,128)(2,1)} reshape(bf16[4,64,16,256]{3,2,1,0:T(8,128)(2,1)} %copy.37) | data formatting | bytes 4194304 | tf_op jit(solution)/shard_map/reshape;reshape | solution.py:69
  131.4 3.2 %fusion.5 = f32[1,4,32,512]{3,2,1,0:T(8,128)} fusion(bf16[4,512,512]{2,1,0:T(8,128)(2,1)} %reshape_reshape.3, f32[1,4,32,512]{3,2,1,0:T(8,128)S(1)} %copy-done.1, pred[4]{0:T(512)(128)(4,1)S(1)} %iota_compare_fusion.1, s32[]{:T(128)S(6)} %select_n.42), kind=kOutput, calls=%fused_computation.8 | convolution fusion | flops 67371008 | bytes 2752520 | tf_op jit(solution)/shard_map/crk,cjk->crj/dot_general | solution.py:76
  134.6 1.8 %fusion.12 = (f32[4]{0:T(128)S(1)}, f32[1,4,32,512]{3,2,1,0:T(8,128)}) fusion(f32[1,4,32,512]{3,2,1,0:T(8,128)S(1)} %copy-done.3, pred[4]{0:T(512)(128)(4,1)S(1)} %iota_compare_fusion.1, bf16[4,512,512]{2,1,0:T(8,128)(2,1)} %reshape_reshape.3, s32[]{:T(128)S(6)} %select_n.42), kind=kLoop, calls=%fused_computation.23 | loop fusion | flops 655356 | bytes 655384 | tf_op jit(solution)/shard_map/reduce_sum | solution.py:101
  136.4 2.5 %multiply_reduce_fusion = (f32[4]{0:T(128)S(1)}, f32[4,32,512]{2,1,0:T(8,128)S(1)}) fusion(bf16[1,4,512,512]{3,2,1,0:T(8,128)(2,1)S(1)} %copy-done, bf16[4,512,512]{2,1,0:T(8,128)(2,1)} %reshape_reshape.3, bf16[1,4,32,512]{3,2,1,0:T(8,128)(2,1)S(1)} %copy-done.4), kind=kOutput, calls=%fused_computation.22 | convolution fusion | flops 134414336 | bytes 4587536 | tf_op jit(solution)/shard_map/crk,ckj->crj/dot_general | solution.py:91
  138.9 0.1 pad_maximum_fusion
  139.0 0.6 broadcast_in_dim.63
  139.6 5.6 %all-to-all-start.3 = ((f32[16,1,8]{2,1,0:T(1,128)}), f32[16,1,8]{2,1,0:T(1,128)S(1)}, u32[]{:S(2)}, u32[]{:S(2)}) async-start(f32[16,1,8]{2,1,0:T(1,128)} %broadcast_in_dim.63), calls=%async_computation.3 | async-start | bytes 16384 | tf_op jit(solution)/shard_map/all_to_all | solution.py:31
  145.2 3.2 %fusion.7 = f32[1,4,32,512]{3,2,1,0:T(8,128)} fusion(bf16[4,512,512]{2,1,0:T(8,128)(2,1)} %reshape_reshape.3, s32[]{:T(128)S(6)} %select_n.42, f32[1,4,32,512]{3,2,1,0:T(8,128)S(1)} %copy-done.2, pred[4]{0:T(512)(128)(4,1)S(1)} %iota_compare_fusion.1), kind=kOutput, calls=%fused_computation.10 | convolution fusion | flops 67371008 | bytes 3145736 | tf_op jit(solution)/shard_map/ckr,ckj->crj/dot_general | solution.py:77
  148.4 3.2 %all-to-all-done.3 = f32[16,1,8]{2,1,0:T(1,128)S(1)} async-done(((f32[16,1,8]{2,1,0:T(1,128)}), f32[16,1,8]{2,1,0:T(1,128)S(1)}, u32[]{:S(2)}, u32[]{:S(2)}) %all-to-all-start.3) | async-done | bytes 544 | tf_op jit(solution)/shard_map/all_to_all | solution.py:31
  151.6 0.6 sqrt_select_fusion
  152.3 0.8 multiply_bitcast_fusion
  (15 shorter events, 0.1 us)
Async XLA Ops:
  0.6 135.7 %copy-start = (bf16[1,4,512,512]{3,2,1,0:T(8,128)(2,1)S(1)}, bf16[1,4,512,512]{3,2,1,0:T(8,128)(2,1)}, u32[]{:S(2)}) copy-start(bf16[1,4,512,512]{3,2,1,0:T(8,128)(2,1)} %param.12) | copy-start | bytes 6291460
  2.7 8.9 %copy-start.5 = (s32[64,4]{0,1:T(4,128)S(1)}, s32[64,4]{0,1:T(4,128)}, u32[]{:S(2)}) copy-start(s32[64,4]{0,1:T(4,128)} %param.14) | copy-start | bytes 3076
  2.8 9.1 %copy-start.6 = (s32[64]{0:T(128)S(1)}, s32[64]{0:T(128)}, u32[]{:S(2)}) copy-start(s32[64]{0:T(128)} %param.15) | copy-start | bytes 772
  4.1 19.3 %all-to-all-start = ((bf16[16,128,256]{2,1,0:T(8,128)(2,1)}), bf16[16,128,256]{2,1,0:T(8,128)(2,1)S(1)}, u32[]{:S(2)}, u32[]{:S(2)}) async-start(bf16[16,128,256]{2,1,0:T(8,128)(2,1)} %copy.34), calls=%async_computation | async-start | bytes 2097152 | tf_op jit(solution)/shard_map/all_to_all | solution.py:19
  92.8 30.4 %all-to-all-start.2 = ((bf16[16,4,64,256]{3,2,1,0:T(8,128)(2,1)}), bf16[16,4,64,256]{3,2,1,0:T(8,128)(2,1)}, u32[]{:S(2)}, u32[]{:S(2)}) async-start(bf16[16,4,64,256]{3,2,1,0:T(8,128)(2,1)} %broadcast_in_dim.59), calls=%async_computation.2 | async-start | bytes 4194304 | tf_op jit(solution)/shard_map/all_to_all | solution.py:31
  127.3 4.1 %copy-start.1 = (f32[1,4,32,512]{3,2,1,0:T(8,128)S(1)}, f32[1,4,32,512]{3,2,1,0:T(8,128)}, u32[]{:S(2)}) copy-start(f32[1,4,32,512]{3,2,1,0:T(8,128)} %param.9) | copy-start | bytes 786436
  131.4 3.2 %copy-start.3 = (f32[1,4,32,512]{3,2,1,0:T(8,128)S(1)}, f32[1,4,32,512]{3,2,1,0:T(8,128)}, u32[]{:S(2)}) copy-start(f32[1,4,32,512]{3,2,1,0:T(8,128)} %param.13) | copy-start | bytes 786436
  131.4 5.0 %copy-start.4 = (bf16[1,4,32,512]{3,2,1,0:T(8,128)(2,1)S(1)}, bf16[1,4,32,512]{3,2,1,0:T(8,128)(2,1)}, u32[]{:S(2)}) copy-start(bf16[1,4,32,512]{3,2,1,0:T(8,128)(2,1)} %param.11) | copy-start | bytes 393220
  136.4 8.9 %copy-start.2 = (f32[1,4,32,512]{3,2,1,0:T(8,128)S(1)}, f32[1,4,32,512]{3,2,1,0:T(8,128)}, u32[]{:S(2)}) copy-start(f32[1,4,32,512]{3,2,1,0:T(8,128)} %param.10) | copy-start | bytes 786436
  139.6 12.0 %all-to-all-start.3 = ((f32[16,1,8]{2,1,0:T(1,128)}), f32[16,1,8]{2,1,0:T(1,128)S(1)}, u32[]{:S(2)}, u32[]{:S(2)}) async-start(f32[16,1,8]{2,1,0:T(1,128)} %broadcast_in_dim.63), calls=%async_computation.3 | async-start | bytes 16384 | tf_op jit(solution)/shard_map/all_to_all | solution.py:31
where the time goes:
time: 156 us; the launch traced here: 153 us
  blocking collectives  66.3 us (42%)
  waiting for transfers between devices  39.4 us (25%)
  starting transfers between devices  17.6 us (11%)
  local copies, waits for them, and re-layouts  15.8 us (10%)
  matrix products  8.88 us (6%)
  other arithmetic  4.28 us (3%)
    all_to_all x1, blocking collectives, on_device(): lax.all_to_all(picked, 'fsdp', split_axis=0, concat_axis=1, tiled=True)  66.3 us
    all_to_all x2, waiting for transfers between devices, sent_to_all(): return lax.all_to_all(copies, axis, split_axis=0, concat_axis=0, tiled=True)  28 us
    all_to_all x1, waiting for transfers between devices, sum_at_owner(): lax.all_to_all(tiles, axis, split_axis=0, concat_axis=0, tiled=True)  11.4 us
    all_to_all x2, starting transfers between devices, sent_to_all(): return lax.all_to_all(copies, axis, split_axis=0, concat_axis=0, tiled=True)  10 us
    all_to_all x1, starting transfers between devices, sum_at_owner(): lax.all_to_all(tiles, axis, split_axis=0, concat_axis=0, tiled=True)  7.57 us
    transpose x1, local copies, waits for them, and re-layouts, joined_along(): return jnp.moveaxis(tiles, 0, dim).reshape(lengths)  4.09 us
    another operation x1, local copies, waits for them, and re-layouts, on_device(): grad_full = gathered.reshape(slot_count, block_order, block_order)  4.08 us
    dot_general x1, matrix products, on_device(): jnp.einsum('ckr,ckj->crj', column_grad, grad_full, preferred_element_type...  3.18 us
  transfers between devices with their start and end apart: 3, of which 3 were waited for; matrix products, arithmetic and copies ran while one was open for 3% of the time, Pallas kernels for 0%

commit v1 on v0

v1 whole, which is shorter than its diff:
```python
import jax
import jax.numpy as jnp
from jax import lax
from jax.experimental import pallas as pl
from jax.experimental.pallas import tpu as pltpu
from jax.sharding import PartitionSpec as P

SHAMPOO_BETA = 0.998
ADAM_BETA = 0.95
EPSILON = 1e-08

SIDE = 4
LANES = 128
PART = LANES // SIDE
F32 = jnp.float32
BF16 = jnp.bfloat16


def kernel(
    n_fsdp,
    slot_ref,
    count_ref,
    grads,
    left_old,
    right_old,
    left_root,
    right_root,
    moment_old,
    left_out,
    right_out,
    moment_out,
    update_out,
    own_tile,
    first_in,
    stacked,
    perm,
    rep,
    second_send,
    second_in,
    table,
    message,
    gathered,
    lo_v,
    ro_v,
    lr_v,
    rr_v,
    mo_v,
    left_v,
    right_v,
    moment_v,
    update_v,
    lhs_v,
    half_v,
    term_v,
    own_v,
    norm_out,
    norm_in,
    load_sem,
    out_sem,
    first_send_sem,
    first_recv_sem,
    second_send_sem,
    second_recv_sem,
    swap_send_sem,
    swap_recv_sem,
    a_send_sem,
    a_recv_sem,
    b_send_sem,
    b_recv_sem,
    norm_send_sem,
    norm_recv_sem,
    from_left,
    from_right,
):
    dp = lax.axis_index("dp")
    owner = lax.axis_index("fsdp")
    gx, gy = dp // SIDE, dp % SIDE
    z, core = owner // 2, owner % 2
    n_z = n_fsdp // 2
    other = 1 - core
    i1 = gx * other + gy * core
    i2 = gy * other + gx * core

    def first_peer(k):
        return (((gx + k * other) % SIDE) * SIDE + (gy + k * core) % SIDE, owner)

    def second_peer(k):
        return (((gx + k * core) % SIDE) * SIDE + (gy + k * other) % SIDE, owner)

    def x_peer(k):
        return (((gx + k) % SIDE) * SIDE + gy, owner)

    def y_peer(k):
        return (gx * SIDE + (gy + k) % SIDE, owner)

    def z_peer(k):
        return (dp, ((z + k + n_z) % n_z) * 2 + core)

    def remote(src, dst, send, recv, peer):
        return pltpu.make_async_remote_copy(
            src_ref=src,
            dst_ref=dst,
            send_sem=send,
            recv_sem=recv,
            device_id=peer,
            device_id_type=pl.DeviceIdType.MESH,
        )

    own_load = pltpu.make_async_copy(
        grads.at[0, :, :, pl.ds(pl.multiple_of(i1 * LANES, LANES), LANES)], own_tile, load_sem.at[0]
    )
    own_load.start()

    barrier = pltpu.get_barrier_semaphore()
    greeted = [x_peer(k) for k in range(1, SIDE)] + [y_peer(k) for k in range(1, SIDE)]
    greeted += [z_peer(1), z_peer(-1), (dp, z * 2 + other)]
    for peer in greeted:
        pl.semaphore_signal(barrier, inc=1, device_id=peer, device_id_type=pl.DeviceIdType.MESH)
    loads = [
        pltpu.make_async_copy(src.at[0], dst, load_sem.at[1 + n])
        for n, (src, dst) in enumerate(
            ((left_old, lo_v), (right_old, ro_v), (left_root, lr_v), (right_root, rr_v), (moment_old, mo_v))
        )
    ]
    for load in loads:
        load.start()
    pl.semaphore_wait(barrier, len(greeted))

    first = []
    for k in (2, 1, 3):
        tile = pl.ds(pl.multiple_of(((i1 + k) % SIDE) * LANES, LANES), LANES)
        copy = remote(
            grads.at[0, :, :, tile],
            first_in.at[k - 1],
            first_send_sem.at[k - 1],
            first_recv_sem.at[k - 1],
            first_peer(k),
        )
        copy.start()
        first.append(copy)

    row = lax.broadcasted_iota(jnp.int32, (SIDE * LANES, SIDE * LANES), 0)
    col = lax.broadcasted_iota(jnp.int32, (SIDE * LANES, SIDE * LANES), 1)
    want = ((col % LANES) // PART) * LANES + (col // LANES) * PART + col % PART
    perm[...] = jnp.where(row == want, 1.0, 0.0).astype(BF16)
    row = lax.broadcasted_iota(jnp.int32, (LANES, SIDE * LANES), 0)
    col = lax.broadcasted_iota(jnp.int32, (LANES, SIDE * LANES), 1)
    rep[...] = jnp.where(row == (col // LANES) * PART + col % PART, 1.0, 0.0).astype(BF16)
    table[pl.ds(SIDE * 32, 1)] = jnp.zeros((1, 8, LANES), F32)

    def meet(step, carry):
        pl.semaphore_signal(from_left, inc=1, device_id=z_peer(1), device_id_type=pl.DeviceIdType.MESH)
        pl.semaphore_signal(from_right, inc=1, device_id=z_peer(-1), device_id_type=pl.DeviceIdType.MESH)
        pl.semaphore_wait(from_left, 1)
        pl.semaphore_wait(from_right, 1)
        return carry

    lax.fori_loop(0, n_z // 2, meet, 0)

    own_load.wait()
    for copy in first:
        copy.wait_recv()
    quads = own_tile.shape[0] // SIDE
    for i in range(SIDE):
        total = own_tile[i * quads : (i + 1) * quads].astype(F32)
        for k in range(SIDE - 1):
            total += first_in[k, i * quads : (i + 1) * quads].astype(F32)
        stacked[:, i * LANES : (i + 1) * LANES] = total.reshape(quads * 8, LANES).astype(BF16)
    packed = jnp.dot(stacked[...], perm[...], preferred_element_type=F32)
    for q in range(SIDE):
        second_send[q] = packed[:, q * LANES : (q + 1) * LANES].astype(BF16)
    second = []
    for k in (2, 1, 3):
        copy = remote(
            second_send.at[(i2 + k) % SIDE],
            second_in.at[k - 1],
            second_send_sem.at[k - 1],
            second_recv_sem.at[k - 1],
            second_peer(k),
        )
        copy.start()
        second.append(copy)
    total = second_send[i2].astype(F32)
    for copy in second:
        copy.wait_recv()
    for k in range(SIDE - 1):
        total += second_in[k].astype(F32)
    spread = jnp.dot(total.astype(BF16), rep[...], preferred_element_type=F32)
    for i in range(SIDE):
        table[i * quads : (i + 1) * quads] = spread[:, i * LANES : (i + 1) * LANES].reshape(quads, 8, LANES)

    lane = lax.broadcasted_iota(jnp.int32, (8, LANES), 1) // PART

    def pick(o, carry):
        held = count_ref[o]
        value = jnp.zeros((8, LANES), F32)
        for s in range(SIDE):
            at = jnp.where(s < held, slot_ref[o, s], SIDE * quads)
            value = jnp.where(lane == s, table[at], value)
        message[o] = value.astype(BF16)
        return carry

    lax.fori_loop(0, n_fsdp, pick, 0)

    mine = i1 * SIDE + i2
    keep = pltpu.make_async_copy(message.at[owner], gathered.at[mine, z, core], swap_recv_sem)
    keep.start()

    def swap(n, carry):
        to = (owner + n + 1) % n_fsdp
        remote(message.at[to], gathered.at[mine, z, core], swap_send_sem, swap_recv_sem, (dp, to)).start()
        return carry

    lax.fori_loop(0, n_fsdp - 1, swap, 0)
    pltpu.make_async_copy(message, message, swap_recv_sem).wait()

    gathers = []
    axes = ((gx, gy, x_peer, y_peer), (gy, gx, y_peer, x_peer))
    for parity, (j1, j2, one, two) in enumerate(axes):
        for k in (2, 1, 3):
            part = gathered.at[j1 * SIDE + j2, :, parity]
            copy = remote(part, part, a_send_sem.at[parity, k - 1], a_recv_sem.at[parity, k - 1], one(k))
            copy.start()
            gathers.append(copy)
        for k in (2, 1, 3):
            part = gathered.at[j1 * SIDE + j2, :, parity]
            copy = remote(part, part, b_send_sem.at[parity, 0, k - 1], b_recv_sem.at[parity, 0, k - 1], two(k))
            copy.start()
            gathers.append(copy)
    late = []
    for k in (1, 3, 2):
        for parity, (j1, j2, one, two) in enumerate(axes):
            part = gathered.at[((j1 + SIDE - k) % SIDE) * SIDE + j2, :, parity]
            remote(part, part, a_send_sem.at[parity, k - 1], a_recv_sem.at[parity, k - 1], one(k)).wait_recv()
            for m in (2, 1, 3):
                copy = remote(part, part, b_send_sem.at[parity, k, m - 1], b_recv_sem.at[parity, k, m - 1], two(m))
                copy.start()
                late.append(copy)
    for parity in range(2):
        for m in range(1, SIDE):
            for k in range(SIDE):
                part = gathered.at[0, :, parity]
                remote(part, part, b_send_sem.at[parity, k, m - 1], b_recv_sem.at[parity, k, m - 1], y_peer(m)).wait_recv()

    for load in loads:
        load.wait()
    order = n_z * 16
    rows = lo_v.shape[1]
    own_rows = pl.ds(2 * dp, 2)

    def piece(p):
        return gathered[p].reshape(order, LANES)

    stack = SIDE * rows
    lhs_v[0:stack] = lr_v[...].reshape(stack, order)
    lhs_v[stack : 2 * stack] = piece(dp).T
    blockdiag = (
        lax.broadcasted_iota(jnp.int32, (stack, LANES), 0) // rows
        == lax.broadcasted_iota(jnp.int32, (stack, LANES), 1) // PART
    )
    lane_part = lax.broadcasted_iota(jnp.int32, (rows, LANES), 1) // PART
    held = count_ref[owner]

    def settle(value, s):
        result = jnp.zeros((rows, LANES), F32)
        for q in range(SIDE):
            block = value[q]
            shift = ((q - s) * PART) % LANES
            if shift:
                block = pltpu.roll(block, shift, axis=1)
            result = jnp.where(lane_part == q, block, result)
        return result

    def column(ct, left_sum):
        pieces = [piece(ct * SIDE + q) for q in range(SIDE)]
        wide = jnp.concatenate(pieces, axis=1)
        both = jnp.dot(lhs_v[...], wide, preferred_element_type=F32)
        mine_rows = [gathered[ct * SIDE + q, own_rows].reshape(rows, LANES) for q in range(SIDE)]
        masked = jnp.concatenate(
            [jnp.where(blockdiag, jnp.concatenate([m.astype(F32)] * SIDE, axis=0), 0.0).astype(BF16) for m in mine_rows],
            axis=1,
        )
        left_sum += lax.dot_general(masked, wide, (((1,), (1,)), ((), ())), preferred_element_type=F32)
        for s in range(SIDE):
            at = slice(s * rows, (s + 1) * rows)
            half_v[ct, at] = settle([both[at, q * LANES : (q + 1) * LANES] for q in range(SIDE)], s).astype(BF16)
            low = slice(stack + s * rows, stack + (s + 1) * rows)
            term_v[ct, at] = settle([both[low, q * LANES : (q + 1) * LANES] for q in range(SIDE)], s)
            own_v[ct, at] = settle([m.astype(F32) for m in mine_rows], s)
        return left_sum

    left_sum = lax.fori_loop(0, SIDE, column, jnp.zeros((stack, order), F32))

    squares = []
    adams = []
    for s in range(SIDE):
        at = slice(s * rows, (s + 1) * rows)
        live = jnp.full((rows, LANES), s, jnp.int32) < jnp.full((rows, LANES), held, jnp.int32)
        precond = jnp.zeros((rows, order), F32)
        for ct in range(SIDE):
            precond += jnp.dot(
                half_v[ct, at], rr_v[s, ct * LANES : (ct + 1) * LANES, :], preferred_element_type=F32
            )
        update_v[s] = precond
        square = precond * precond
        lanes_sum = jnp.zeros((rows, LANES), F32)
        adam_sum = jnp.zeros((rows, LANES), F32)
        for ct in range(SIDE):
            here = slice(ct * LANES, (ct + 1) * LANES)
            lanes_sum += square[:, here]
            value = own_v[ct, at]
            old = mo_v[s, :, here]
            new = jnp.where(live, ADAM_BETA * old + (1.0 - ADAM_BETA) * value * value, old)
            moment_v[s, :, here] = new
            adam = value / (jnp.sqrt(new) + EPSILON)
            adam_sum += adam * adam
            old = lo_v[s, :, here]
            left_v[s, :, here] = jnp.where(
                live, SHAMPOO_BETA * old + (1.0 - SHAMPOO_BETA) * left_sum[at, here], old
            )
            old = ro_v[s, :, here]
            right_v[s, :, here] = jnp.where(
                live, SHAMPOO_BETA * old + (1.0 - SHAMPOO_BETA) * term_v[ct, at], old
            )
        squares.append(jnp.sum(lanes_sum, axis=0, keepdims=True))
        adams.append(jnp.sum(adam_sum, axis=0, keepdims=True))
    norms = jnp.concatenate(squares + adams, axis=0)
    norm_out[...] = norms

    n_dp = SIDE * SIDE

    def share(n, carry):
        to = ((dp + n + 1) % n_dp, owner)
        remote(norm_out, norm_in.at[n], norm_send_sem, norm_recv_sem, to).start()
        return carry

    lax.fori_loop(0, n_dp - 1, share, 0)
    outs = [
        pltpu.make_async_copy(src, dst.at[0], out_sem.at[n])
        for n, (src, dst) in enumerate(((left_v, left_out), (right_v, right_out), (moment_v, moment_out)))
    ]
    for copy in outs:
        copy.start()
    pltpu.make_async_copy(norm_in, norm_in, norm_recv_sem).wait()
    for n in range(n_dp - 1):
        norms += norm_in[n]
    sums = jnp.broadcast_to(jnp.sum(norms, axis=1, keepdims=True), (8, LANES))
    slot = lax.broadcasted_iota(jnp.int32, (SIDE, LANES), 0)
    live = slot < jnp.full((SIDE, LANES), held, jnp.int32)
    scale = jnp.where(live, jnp.sqrt(sums[SIDE:] / jnp.where(live, sums[:SIDE], 1.0)), 0.0)
    for s in range(SIDE):
        wide = jnp.broadcast_to(jnp.concatenate([scale[s : s + 1]] * SIDE, axis=1), (rows, order))
        update_v[s] = update_v[s] * wide
    last = pltpu.make_async_copy(update_v, update_out.at[0], out_sem.at[3])
    last.start()
    for copy in first + second + gathers + late:
        copy.wait_send()
    pltpu.make_async_copy(
        message.at[pl.ds(0, n_fsdp - 1)], message.at[pl.ds(0, n_fsdp - 1)], swap_send_sem
    ).wait()
    pltpu.make_async_copy(norm_in, norm_in, norm_send_sem).wait()
    for copy in outs + [last]:
        copy.wait()


def on_device(
    grads, left_stats, right_stats, left_root, right_root, second_moment, slot_block, counts
):
    n_fsdp = lax.axis_size("fsdp")
    n_z = n_fsdp // 2
    blocks, slab = grads.shape[1:3]
    slots, rows, order = left_stats.shape[1:]
    quads = blocks // SIDE
    stack = slots * rows
    blocks = blocks
    hbm = pl.BlockSpec(memory_space=pl.ANY)
    smem = pl.BlockSpec(memory_space=pltpu.SMEM)
    out = jax.ShapeDtypeStruct(left_stats.shape, F32)
    dma = pltpu.SemaphoreType.DMA
    vmem = pltpu.VMEM
    n_dp = SIDE * SIDE
    import functools

    return tuple(
        pl.pallas_call(
            functools.partial(kernel, n_fsdp),
            out_shape=(out,) * 4,
            in_specs=[smem, smem] + [hbm] * 6,
            out_specs=(hbm,) * 4,
            scratch_shapes=[
                vmem((blocks, slab, LANES), BF16),
                vmem((SIDE - 1, blocks, slab, LANES), BF16),
                vmem((quads * slab, SIDE * LANES), BF16),
                vmem((SIDE * LANES, SIDE * LANES), BF16),
                vmem((LANES, SIDE * LANES), BF16),
                vmem((SIDE, quads * slab, LANES), BF16),
                vmem((SIDE - 1, quads * slab, LANES), BF16),
                vmem((blocks + 1, slab, LANES), F32),
                vmem((n_fsdp, slab, LANES), BF16),
                vmem((n_dp, n_z, 2, slab, LANES), BF16),
                vmem((slots, rows, order), F32),
                vmem((slots, rows, order), F32),
                vmem((slots, rows, order), BF16),
                vmem((slots, order, order), BF16),
                vmem((slots, rows, order), F32),
                vmem((slots, rows, order), F32),
                vmem((slots, rows, order), F32),
                vmem((slots, rows, order), F32),
                vmem((slots, rows, order), F32),
                vmem((2 * stack, order), BF16),
                vmem((SIDE, stack, LANES), BF16),
                vmem((SIDE, stack, LANES), F32),
                vmem((SIDE, stack, LANES), F32),
                vmem((8, LANES), F32),
                vmem((n_dp - 1, 8, LANES), F32),
                dma((6,)),
                dma((4,)),
                dma((SIDE - 1,)),
                dma((SIDE - 1,)),
                dma((SIDE - 1,)),
                dma((SIDE - 1,)),
                dma,
                dma,
                dma((2, SIDE - 1)),
                dma((2, SIDE - 1)),
                dma((2, SIDE, SIDE - 1)),
                dma((2, SIDE, SIDE - 1)),
                dma,
                dma,
                pltpu.SemaphoreType.REGULAR,
                pltpu.SemaphoreType.REGULAR,
            ],
            compiler_params=pltpu.CompilerParams(
                collective_id=0, has_side_effects=True, vmem_limit_bytes=48 << 20
            ),
            name="shampoo",
        )(slot_block, counts, grads, left_stats, right_stats, left_root, right_root, second_moment)
    )


def solution(mesh):
    in_specs = (
        P("dp", None, "fsdp", None),
        P("fsdp", None, "dp", None),
        P("fsdp", None, "dp", None),
        P("fsdp", None, "dp", None),
        P("fsdp", None, None, None),
        P("fsdp", None, "dp", None),
        P(),
        P(),
    )
    out_specs = (
        P("fsdp", None, "dp", None),
        P("fsdp", None, "dp", None),
        P("fsdp", None, "dp", None),
        P("fsdp", None, "dp", None),
    )
    return jax.shard_map(
        on_device, mesh=mesh, in_specs=in_specs, out_specs=out_specs, check_vma=False
    )
```

time: 156 us -> 109 us (0.70)
  Pallas kernels: 0 us -> 95.8 us
  blocking collectives: 66.3 us -> 0 us
  waiting for transfers between devices: 39.4 us -> 0 us
  starting transfers between devices: 17.6 us -> 0 us
  matrix products: 8.88 us -> 0 us
  local copies, waits for them, and re-layouts: 15.8 us -> 10.8 us
  other arithmetic: 4.28 us -> 0 us
    pallas_call x0 -> x1, Pallas kernels: none -> 95.8 us  [on_device(): pl.pallas_call(functools.partial(kernel, n_fsdp), out_shape=(out,) * 4, i...]
    all_to_all x1 -> x0, blocking collectives: 66.3 us -> none  [on_device(): lax.all_to_all(picked, 'fsdp', split_axis=0, concat_axis=1, tiled=True)]
    all_to_all x3 -> x0, waiting for transfers between devices: 39.4 us -> none  [the longest x2 28 us: sent_to_all(): return lax.all_to_all(copies, axis, split_axis=0, concat_axis=0, tiled=True)]
    all_to_all x3 -> x0, starting transfers between devices: 17.6 us -> none  [the longest x2 10 us: sent_to_all(): return lax.all_to_all(copies, axis, split_axis=0, concat_axis=0, tiled=True)]
    dot_general x3 -> x0, matrix products: 8.88 us -> none  [the longest x1 3.18 us: on_device(): jnp.einsum('ckr,ckj->crj', column_grad, grad_full, preferred_element_type...]
    unnamed x16 -> x19, local copies, waits for them, and re-layouts: 2.22 us -> 10.8 us
    transpose x2 -> x0, local copies, waits for them, and re-layouts: 5.39 us -> none  [the longest x1 4.09 us: joined_along(): return jnp.moveaxis(tiles, 0, dim).reshape(lengths)]
    another operation x1 -> x0, local copies, waits for them, and re-layouts: 4.08 us -> none  [on_device(): grad_full = gathered.reshape(slot_count, block_order, block_order)]
  transfers between devices with their start and end apart: 3 -> 0, of which waited for: 3 -> 0; matrix products, arithmetic and copies ran while one was open for 3% -> 0% of each run, Pallas kernels for 0% -> 0%
where the time goes in v1:
time: 109 us; the launch traced here: 107 us
  Pallas kernels  95.8 us (88%)
  local copies, waits for them, and re-layouts  10.8 us (10%)
    pallas_call x1, Pallas kernels, on_device(): pl.pallas_call(functools.partial(kernel, n_fsdp), out_shape=(out,) * 4, i...  95.8 us
    unnamed x19, local copies, waits for them, and re-layouts  10.8 us

profile of v1, /device:TPU:1, one launch (start us, length us, event | category | flops | bytes accessed | tf_op | source)
XLA Modules:
  0.0 107.3 jit_solution(12204292005139947079)
XLA Ops:
  0.6 0.8 copy.12.slot_ref
  1.4 0.0 copy-start
  1.4 1.6 %copy-done = bf16[1,4,512,512]{3,2,1,0:T(8,128)(2,1)S(1)} copy-done((bf16[1,4,512,512]{3,2,1,0:T(8,128)(2,1)S(1)}, bf16[1,4,512,512]{3,2,1,0:T(8,128)(2,1)}, u32[]{:S(2)}) %copy-start) | copy-done | bytes 2097176
  3.0 0.0 copy-start.1
  3.0 1.2 %copy-done.1 = bf16[1,128,8,512]{3,2,1,0:T(8,128)(2,1)S(1)} copy-done((bf16[1,128,8,512]{3,2,1,0:T(8,128)(2,1)S(1)}, bf16[1,128,8,512]{3,2,1,0:T(8,128)(2,1)}, u32[]{:S(2)}) %copy-start.1) | copy-done | bytes 1048600
  4.2 0.0 copy-start.2
  4.2 0.9 copy-done.2
  5.2 0.0 copy-start.3
  5.2 0.9 copy-done.3
  6.1 0.0 copy-start.4
  6.1 0.9 copy-done.4
  7.1 0.0 copy-start.5
  7.1 0.9 copy-done.5
  8.0 0.0 copy-start.6
  8.0 0.7 copy-done.6
  8.6 95.8 %shampoo.1 = (f32[1,4,32,512]{3,2,1,0:T(8,128)S(1)}, f32[1,4,32,512]{3,2,1,0:T(8,128)S(1)}, f32[1,4,32,512]{3,2,1,0:T(8,128)S(1)}, f32[1,4,32,512]{3,2,1,0:T(8,128)S(1)}) custom-call(s32[64,4]{1,0:T(8,128)S(1)} %copy.12.slot_ref, s32[64]{0:T(128)S(1)} %copy-done.6, bf16[1,128,8,512]{3,2,1,0:T(8,128)(2,1)S(1)} %copy-done.1, f32[1,4,32,512]{3,2,1,0:T(8,128)S(1)} %copy-done.2, ...), custom_call_target="tpu_custom_call" | custom-call | tf_op jit(solution)/shard_map/shampoo/pallas_call | solution.py:385
  104.5 0.7 copy.17
  105.2 0.7 copy.18
  105.9 0.7 copy.19
  106.6 0.7 copy.20
Async XLA Ops:
  1.4 1.6 %copy-start = (bf16[1,4,512,512]{3,2,1,0:T(8,128)(2,1)S(1)}, bf16[1,4,512,512]{3,2,1,0:T(8,128)(2,1)}, u32[]{:S(2)}) copy-start(bf16[1,4,512,512]{3,2,1,0:T(8,128)(2,1)} %right_root.1) | copy-start | bytes 6291460
  3.0 1.2 %copy-start.1 = (bf16[1,128,8,512]{3,2,1,0:T(8,128)(2,1)S(1)}, bf16[1,128,8,512]{3,2,1,0:T(8,128)(2,1)}, u32[]{:S(2)}) copy-start(bf16[1,128,8,512]{3,2,1,0:T(8,128)(2,1)} %grads.1) | copy-start | bytes 3145732
  4.2 0.9 copy-start.2
  5.2 0.9 copy-start.3
  6.1 0.9 copy-start.4
  7.1 0.9 copy-start.5
  8.0 0.7 copy-start.6

commit v2 on v1

--- a/solution.py
+++ b/solution.py
@@ -11,6 +11,7 @@
 
 SIDE = 4
 LANES = 128
+ZONE = 8
 PART = LANES // SIDE
 F32 = jnp.float32
 BF16 = jnp.bfloat16
@@ -69,8 +70,7 @@
     b_recv_sem,
     norm_send_sem,
     norm_recv_sem,
-    from_left,
-    from_right,
+    met,
 ):
     dp = lax.axis_index("dp")
     owner = lax.axis_index("fsdp")
@@ -113,7 +113,10 @@
 
     barrier = pltpu.get_barrier_semaphore()
     greeted = [x_peer(k) for k in range(1, SIDE)] + [y_peer(k) for k in range(1, SIDE)]
-    greeted += [z_peer(1), z_peer(-1), (dp, z * 2 + other)]
+    for k in (0, 1, -1, 2, -2):
+        for c in (core, other):
+            if k or c is other:
+                greeted.append((dp, ((z + k + n_z) % n_z) * 2 + c))
     for peer in greeted:
         pl.semaphore_signal(barrier, inc=1, device_id=peer, device_id_type=pl.DeviceIdType.MESH)
     loads = [
@@ -148,14 +151,22 @@
     rep[...] = jnp.where(row == (col // LANES) * PART + col % PART, 1.0, 0.0).astype(BF16)
     table[pl.ds(SIDE * 32, 1)] = jnp.zeros((1, 8, LANES), F32)
 
-    def meet(step, carry):
-        pl.semaphore_signal(from_left, inc=1, device_id=z_peer(1), device_id_type=pl.DeviceIdType.MESH)
-        pl.semaphore_signal(from_right, inc=1, device_id=z_peer(-1), device_id_type=pl.DeviceIdType.MESH)
-        pl.semaphore_wait(from_left, 1)
-        pl.semaphore_wait(from_right, 1)
-        return carry
-
-    lax.fori_loop(0, n_z // 2, meet, 0)
+    reach = []
+    k = 2
+    while k < n_z // 2:
+        reach.append(k)
+        k *= 2
+
+    def tell(n):
+        for k in (reach[n], -reach[n]):
+            pl.semaphore_signal(
+                met.at[n], inc=1, device_id=z_peer(k), device_id_type=pl.DeviceIdType.MESH
+            )
+
+    tell(0)
+    for n in range(1, len(reach)):
+        pl.semaphore_wait(met.at[n - 1], 2)
+        tell(n)
 
     own_load.wait()
     for copy in first:
@@ -202,45 +213,67 @@
 
     lax.fori_loop(0, n_fsdp, pick, 0)
 
+    pl.semaphore_wait(met.at[len(reach) - 1], 2)
     mine = i1 * SIDE + i2
-    keep = pltpu.make_async_copy(message.at[owner], gathered.at[mine, z, core], swap_recv_sem)
+    zone = z // ZONE
+    keep = pltpu.make_async_copy(message.at[owner], gathered.at[mine, z, core], swap_recv_sem.at[zone])
     keep.start()
 
+    def send_to(to):
+        remote(
+            message.at[to], gathered.at[mine, z, core], swap_send_sem, swap_recv_sem.at[zone], (dp, to)
+        ).start()
+
+    send_to(z * 2 + other)
+
     def swap(n, carry):
-        to = (owner + n + 1) % n_fsdp
-        remote(message.at[to], gathered.at[mine, z, core], swap_send_sem, swap_recv_sem, (dp, to)).start()
+        for step in (n + 1, n_z - 1 - n):
+            for c in range(2):
+                send_to(((z + step) % n_z) * 2 + c)
         return carry
 
-    lax.fori_loop(0, n_fsdp - 1, swap, 0)
-    pltpu.make_async_copy(message, message, swap_recv_sem).wait()
-
-    gathers = []
+    lax.fori_loop(0, n_z // 2 - 1, swap, 0)
+    for c in range(2):
+        send_to(((z + n_z // 2) % n_z) * 2 + c)
+
     axes = ((gx, gy, x_peer, y_peer), (gy, gx, y_peer, x_peer))
-    for parity, (j1, j2, one, two) in enumerate(axes):
+    zones = n_z // ZONE
+
+    def along(parity, n, k, m, j1_back):
+        j1, j2, one, two = axes[parity]
+        at = pl.ds(pl.multiple_of(((zone + near_first[n]) % zones) * ZONE, ZONE), ZONE)
+        part = gathered.at[((j1 + SIDE - j1_back) % SIDE) * SIDE + j2, at, parity]
+        if m:
+            return remote(part, part, b_send_sem, b_recv_sem, two(m))
+        return remote(part, part, a_send_sem, a_recv_sem.at[n, parity, k - 1], one(k))
+
+    near_first = (0, 1, zones - 1, 2)
+
+    def first_gather(n):
+        here = (zone + near_first[n]) % zones
+        whole = message.at[pl.ds(0, 2 * ZONE)]
+        pltpu.make_async_copy(whole, whole, swap_recv_sem.at[here]).wait()
         for k in (2, 1, 3):
-            part = gathered.at[j1 * SIDE + j2, :, parity]
-            copy = remote(part, part, a_send_sem.at[parity, k - 1], a_recv_sem.at[parity, k - 1], one(k))
-            copy.start()
-            gathers.append(copy)
-        for k in (2, 1, 3):
-            part = gathered.at[j1 * SIDE + j2, :, parity]
-            copy = remote(part, part, b_send_sem.at[parity, 0, k - 1], b_recv_sem.at[parity, 0, k - 1], two(k))
-            copy.start()
-            gathers.append(copy)
-    late = []
-    for k in (1, 3, 2):
-        for parity, (j1, j2, one, two) in enumerate(axes):
-            part = gathered.at[((j1 + SIDE - k) % SIDE) * SIDE + j2, :, parity]
-            remote(part, part, a_send_sem.at[parity, k - 1], a_recv_sem.at[parity, k - 1], one(k)).wait_recv()
-            for m in (2, 1, 3):
-                copy = remote(part, part, b_send_sem.at[parity, k, m - 1], b_recv_sem.at[parity, k, m - 1], two(m))
-                copy.start()
-                late.append(copy)
-    for parity in range(2):
-        for m in range(1, SIDE):
-            for k in range(SIDE):
-                part = gathered.at[0, :, parity]
-                remote(part, part, b_send_sem.at[parity, k, m - 1], b_recv_sem.at[parity, k, m - 1], y_peer(m)).wait_recv()
+            for parity in range(2):
+                along(parity, n, k, 0, 0).start()
+        for m in (2, 1, 3):
+            for parity in range(2):
+                along(parity, n, 0, m, 0).start()
+
+    def second_gather(n):
+        for k in (1, 3, 2):
+            for parity in range(2):
+                along(parity, n, k, 0, k).wait_recv()
+                for m in (2, 1, 3):
+                    along(parity, n, k, m, k).start()
+
+    for n in range(zones):
+        first_gather(n)
+        if n:
+            second_gather(n - 1)
+    second_gather(zones - 1)
+    third = gathered.at[pl.ds(0, SIDE * (SIDE - 1))]
+    pltpu.make_async_copy(third, third, b_recv_sem).wait()
 
     for load in loads:
         load.wait()
@@ -290,6 +323,8 @@
         return left_sum
 
     left_sum = lax.fori_loop(0, SIDE, column, jnp.zeros((stack, order), F32))
+    for s in range(SIDE):
+        left_v[s] = left_sum[s * rows : (s + 1) * rows]
 
     squares = []
     adams = []
@@ -314,27 +349,32 @@
             moment_v[s, :, here] = new
             adam = value / (jnp.sqrt(new) + EPSILON)
             adam_sum += adam * adam
+        squares.append(jnp.sum(lanes_sum, axis=0, keepdims=True))
+        adams.append(jnp.sum(adam_sum, axis=0, keepdims=True))
+    norms = jnp.concatenate(squares + adams, axis=0)
+    norm_out[...] = norms
+
+    n_dp = SIDE * SIDE
+
+    def share(n, carry):
+        to = ((dp + n + 1) % n_dp, owner)
+        remote(norm_out, norm_in.at[n], norm_send_sem, norm_recv_sem, to).start()
+        return carry
+
+    lax.fori_loop(0, n_dp - 1, share, 0)
+    for s in range(SIDE):
+        at = slice(s * rows, (s + 1) * rows)
+        live = jnp.full((rows, LANES), s, jnp.int32) < jnp.full((rows, LANES), held, jnp.int32)
+        for ct in range(SIDE):
+            here = slice(ct * LANES, (ct + 1) * LANES)
             old = lo_v[s, :, here]
             left_v[s, :, here] = jnp.where(
-                live, SHAMPOO_BETA * old + (1.0 - SHAMPOO_BETA) * left_sum[at, here], old
+                live, SHAMPOO_BETA * old + (1.0 - SHAMPOO_BETA) * left_v[s, :, here], old
             )
             old = ro_v[s, :, here]
             right_v[s, :, here] = jnp.where(
                 live, SHAMPOO_BETA * old + (1.0 - SHAMPOO_BETA) * term_v[ct, at], old
             )
-        squares.append(jnp.sum(lanes_sum, axis=0, keepdims=True))
-        adams.append(jnp.sum(adam_sum, axis=0, keepdims=True))
-    norms = jnp.concatenate(squares + adams, axis=0)
-    norm_out[...] = norms
-
-    n_dp = SIDE * SIDE
-
-    def share(n, carry):
-        to = ((dp + n + 1) % n_dp, owner)
-        remote(norm_out, norm_in.at[n], norm_send_sem, norm_recv_sem, to).start()
-        return carry
-
-    lax.fori_loop(0, n_dp - 1, share, 0)
     outs = [
         pltpu.make_async_copy(src, dst.at[0], out_sem.at[n])
         for n, (src, dst) in enumerate(((left_v, left_out), (right_v, right_out), (moment_v, moment_out)))
@@ -353,8 +393,11 @@
         update_v[s] = update_v[s] * wide
     last = pltpu.make_async_copy(update_v, update_out.at[0], out_sem.at[3])
     last.start()
-    for copy in first + second + gathers + late:
+    for copy in first + second:
         copy.wait_send()
+    sent = gathered.at[pl.ds(0, SIDE - 1)]
+    pltpu.make_async_copy(sent, sent, a_send_sem).wait()
+    pltpu.make_async_copy(third, third, b_send_sem).wait()
     pltpu.make_async_copy(
         message.at[pl.ds(0, n_fsdp - 1)], message.at[pl.ds(0, n_fsdp - 1)], swap_send_sem
     ).wait()
@@ -420,18 +463,17 @@
                 dma((SIDE - 1,)),
                 dma((SIDE - 1,)),
                 dma,
+                dma((n_z // ZONE,)),
                 dma,
-                dma((2, SIDE - 1)),
-                dma((2, SIDE - 1)),
-                dma((2, SIDE, SIDE - 1)),
-                dma((2, SIDE, SIDE - 1)),
+                dma((n_z // ZONE, 2, SIDE - 1)),
                 dma,
                 dma,
-                pltpu.SemaphoreType.REGULAR,
-                pltpu.SemaphoreType.REGULAR,
+                dma,
+                dma,
+                pltpu.SemaphoreType.REGULAR((4,)),
             ],
             compiler_params=pltpu.CompilerParams(
-                collective_id=0, has_side_effects=True, vmem_limit_bytes=48 << 20
+                collective_id=0, has_side_effects=True, vmem_limit_bytes=67043328
             ),
             name="shampoo",
         )(slot_block, counts, grads, left_stats, right_stats, left_root, right_root, second_moment)

time: 109 us -> 87.3 us (0.80); the launches traced: 107 us -> 86.9 us
  Pallas kernels: 95.8 us -> 78.1 us
  local copies, waits for them, and re-layouts: 10.8 us -> 8.07 us
    pallas_call x1, Pallas kernels: 95.8 us -> 78.1 us  [on_device(): pl.pallas_call(functools.partial(kernel, n_fsdp), out_shape=(out,) * 4, i...]
    unnamed x19 -> x5, local copies, waits for them, and re-layouts: 10.8 us -> 8.07 us
where the time goes in v2:
time: 87.3 us; the launch traced here: 86.9 us
  Pallas kernels  78.1 us (89%)
  local copies, waits for them, and re-layouts  8.07 us (9%)
    pallas_call x1, Pallas kernels, on_device(): pl.pallas_call(functools.partial(kernel, n_fsdp), out_shape=(out,) * 4, i...  78.1 us
    unnamed x5, local copies, waits for them, and re-layouts  8.07 us

profile of v2, /device:TPU:1, one launch (start us, length us, event | category | flops | bytes accessed | tf_op | source)
XLA Modules:
  0.0 86.9 jit_solution(1132193618582670542)
XLA Ops:
  0.6 1.4 %copy.12.slot_ref = s32[64,4]{1,0:T(8,128)} copy(s32[64,4]{0,1:T(4,128)} %param.14) | data formatting | bytes 2048 | tf_op args[6]
  2.0 78.1 %shampoo.1 = (f32[1,4,32,512]{3,2,1,0:T(8,128)}, f32[1,4,32,512]{3,2,1,0:T(8,128)}, f32[1,4,32,512]{3,2,1,0:T(8,128)}, f32[1,4,32,512]{3,2,1,0:T(8,128)}) custom-call(s32[64,4]{1,0:T(8,128)} %copy.12.slot_ref, s32[64]{0:T(128)} %count_ref.1, bf16[1,128,8,512]{3,2,1,0:T(8,128)(2,1)} %grads.1, f32[1,4,32,512]{3,2,1,0:T(8,128)} %left_old.1, ...), custom_call_target="tpu_custom_call" | custom-call | tf_op jit(solution)/shard_map/shampoo/pallas_call | solution.py:428
  80.2 1.7 %copy.17 = f32[1,4,32,512]{3,2,1,0:T(8,128)} copy(f32[1,4,32,512]{3,2,1,0:T(8,128)} %get-tuple-element.8) | data formatting | bytes 524288
  81.8 1.7 %copy.18 = f32[1,4,32,512]{3,2,1,0:T(8,128)} copy(f32[1,4,32,512]{3,2,1,0:T(8,128)} %get-tuple-element.9) | data formatting | bytes 524288
  83.5 1.7 %copy.19 = f32[1,4,32,512]{3,2,1,0:T(8,128)} copy(f32[1,4,32,512]{3,2,1,0:T(8,128)} %get-tuple-element.10) | data formatting | bytes 524288
  85.2 1.7 %copy.20 = f32[1,4,32,512]{3,2,1,0:T(8,128)} copy(f32[1,4,32,512]{3,2,1,0:T(8,128)} %get-tuple-element.11) | data formatting | bytes 524288

commit v3 on v2

--- a/solution.py
+++ b/solution.py
@@ -1,3 +1,5 @@
+import functools
+
 import jax
 import jax.numpy as jnp
 from jax import lax
@@ -11,7 +13,7 @@
 
 SIDE = 4
 LANES = 128
-ZONE = 8
+SPAN = 4
 PART = LANES // SIDE
 F32 = jnp.float32
 BF16 = jnp.bfloat16
@@ -19,6 +21,7 @@
 
 def kernel(
     n_fsdp,
+    span,
     slot_ref,
     count_ref,
     grads,
@@ -31,6 +34,7 @@
     right_out,
     moment_out,
     update_out,
+    scale_out,
     own_tile,
     first_in,
     stacked,
@@ -56,6 +60,7 @@
     own_v,
     norm_out,
     norm_in,
+    scale_v,
     load_sem,
     out_sem,
     first_send_sem,
@@ -206,16 +211,16 @@
         held = count_ref[o]
         value = jnp.zeros((8, LANES), F32)
         for s in range(SIDE):
-            at = jnp.where(s < held, slot_ref[o, s], SIDE * quads)
+            at = jnp.where(s < held, slot_ref[s, o], SIDE * quads)
             value = jnp.where(lane == s, table[at], value)
         message[o] = value.astype(BF16)
         return carry
 
-    lax.fori_loop(0, n_fsdp, pick, 0)
+    lax.fori_loop(0, n_fsdp, pick, 0, unroll=4)
 
     pl.semaphore_wait(met.at[len(reach) - 1], 2)
     mine = i1 * SIDE + i2
-    zone = z // ZONE
+    zone = z // span
     keep = pltpu.make_async_copy(message.at[owner], gathered.at[mine, z, core], swap_recv_sem.at[zone])
     keep.start()
 
@@ -232,26 +237,26 @@
                 send_to(((z + step) % n_z) * 2 + c)
         return carry
 
-    lax.fori_loop(0, n_z // 2 - 1, swap, 0)
+    lax.fori_loop(0, n_z // 2 - 1, swap, 0, unroll=5)
     for c in range(2):
         send_to(((z + n_z // 2) % n_z) * 2 + c)
 
     axes = ((gx, gy, x_peer, y_peer), (gy, gx, y_peer, x_peer))
-    zones = n_z // ZONE
+    zones = n_z // span
 
     def along(parity, n, k, m, j1_back):
         j1, j2, one, two = axes[parity]
-        at = pl.ds(pl.multiple_of(((zone + near_first[n]) % zones) * ZONE, ZONE), ZONE)
+        at = pl.ds(pl.multiple_of(((zone + near_first[n]) % zones) * span, span), span)
         part = gathered.at[((j1 + SIDE - j1_back) % SIDE) * SIDE + j2, at, parity]
         if m:
             return remote(part, part, b_send_sem, b_recv_sem, two(m))
         return remote(part, part, a_send_sem, a_recv_sem.at[n, parity, k - 1], one(k))
 
-    near_first = (0, 1, zones - 1, 2)
+    near_first = sorted(range(zones), key=lambda n: min(n, zones - n))
 
     def first_gather(n):
         here = (zone + near_first[n]) % zones
-        whole = message.at[pl.ds(0, 2 * ZONE)]
+        whole = message.at[pl.ds(0, 2 * span)]
         pltpu.make_async_copy(whole, whole, swap_recv_sem.at[here]).wait()
         for k in (2, 1, 3):
             for parity in range(2):
@@ -285,8 +290,6 @@
         return gathered[p].reshape(order, LANES)
 
     stack = SIDE * rows
-    lhs_v[0:stack] = lr_v[...].reshape(stack, order)
-    lhs_v[stack : 2 * stack] = piece(dp).T
     blockdiag = (
         lax.broadcasted_iota(jnp.int32, (stack, LANES), 0) // rows
         == lax.broadcasted_iota(jnp.int32, (stack, LANES), 1) // PART
@@ -304,27 +307,38 @@
             result = jnp.where(lane_part == q, block, result)
         return result
 
-    def column(ct, left_sum):
-        pieces = [piece(ct * SIDE + q) for q in range(SIDE)]
-        wide = jnp.concatenate(pieces, axis=1)
+    def own_part(ct):
+        return [gathered[ct * SIDE + q, own_rows].reshape(rows, LANES) for q in range(SIDE)]
+
+    def wide_part(ct):
+        return jnp.concatenate([piece(ct * SIDE + q) for q in range(SIDE)], axis=1)
+
+    def halves(ct, carry):
+        both = jnp.dot(lr_v[...].reshape(stack, order), wide_part(ct), preferred_element_type=F32)
+        mine_rows = own_part(ct)
+        for s in range(SIDE):
+            at = slice(s * rows, (s + 1) * rows)
+            half_v[ct, at] = settle([both[at, q * LANES : (q + 1) * LANES] for q in range(SIDE)], s).astype(BF16)
+            own_v[ct, at] = settle([m.astype(F32) for m in mine_rows], s)
+        return carry
+
+    lax.fori_loop(0, SIDE, halves, 0)
+
+    def terms(ct, left_sum):
+        wide = wide_part(ct)
         both = jnp.dot(lhs_v[...], wide, preferred_element_type=F32)
-        mine_rows = [gathered[ct * SIDE + q, own_rows].reshape(rows, LANES) for q in range(SIDE)]
         masked = jnp.concatenate(
-            [jnp.where(blockdiag, jnp.concatenate([m.astype(F32)] * SIDE, axis=0), 0.0).astype(BF16) for m in mine_rows],
+            [
+                jnp.where(blockdiag, jnp.concatenate([m.astype(F32)] * SIDE, axis=0), 0.0).astype(BF16)
+                for m in own_part(ct)
+            ],
             axis=1,
         )
         left_sum += lax.dot_general(masked, wide, (((1,), (1,)), ((), ())), preferred_element_type=F32)
         for s in range(SIDE):
             at = slice(s * rows, (s + 1) * rows)
-            half_v[ct, at] = settle([both[at, q * LANES : (q + 1) * LANES] for q in range(SIDE)], s).astype(BF16)
-            low = slice(stack + s * rows, stack + (s + 1) * rows)
-            term_v[ct, at] = settle([both[low, q * LANES : (q + 1) * LANES] for q in range(SIDE)], s)
-            own_v[ct, at] = settle([m.astype(F32) for m in mine_rows], s)
+            term_v[ct, at] = settle([both[at, q * LANES : (q + 1) * LANES] for q in range(SIDE)], s)
         return left_sum
-
-    left_sum = lax.fori_loop(0, SIDE, column, jnp.zeros((stack, order), F32))
-    for s in range(SIDE):
-        left_v[s] = left_sum[s * rows : (s + 1) * rows]
 
     squares = []
     adams = []
@@ -362,6 +376,8 @@
         return carry
 
     lax.fori_loop(0, n_dp - 1, share, 0)
+    lhs_v[...] = piece(dp).T
+    left_sum = lax.fori_loop(0, SIDE, terms, jnp.zeros((stack, order), F32))
     for s in range(SIDE):
         at = slice(s * rows, (s + 1) * rows)
         live = jnp.full((rows, LANES), s, jnp.int32) < jnp.full((rows, LANES), held, jnp.int32)
@@ -369,7 +385,7 @@
             here = slice(ct * LANES, (ct + 1) * LANES)
             old = lo_v[s, :, here]
             left_v[s, :, here] = jnp.where(
-                live, SHAMPOO_BETA * old + (1.0 - SHAMPOO_BETA) * left_v[s, :, here], old
+                live, SHAMPOO_BETA * old + (1.0 - SHAMPOO_BETA) * left_sum[at, here], old
             )
             old = ro_v[s, :, here]
             right_v[s, :, here] = jnp.where(
@@ -377,7 +393,9 @@
             )
     outs = [
         pltpu.make_async_copy(src, dst.at[0], out_sem.at[n])
-        for n, (src, dst) in enumerate(((left_v, left_out), (right_v, right_out), (moment_v, moment_out)))
+        for n, (src, dst) in enumerate(
+            ((left_v, left_out), (right_v, right_out), (moment_v, moment_out), (update_v, update_out))
+        )
     ]
     for copy in outs:
         copy.start()
@@ -388,10 +406,8 @@
     slot = lax.broadcasted_iota(jnp.int32, (SIDE, LANES), 0)
     live = slot < jnp.full((SIDE, LANES), held, jnp.int32)
     scale = jnp.where(live, jnp.sqrt(sums[SIDE:] / jnp.where(live, sums[:SIDE], 1.0)), 0.0)
-    for s in range(SIDE):
-        wide = jnp.broadcast_to(jnp.concatenate([scale[s : s + 1]] * SIDE, axis=1), (rows, order))
-        update_v[s] = update_v[s] * wide
-    last = pltpu.make_async_copy(update_v, update_out.at[0], out_sem.at[3])
+    scale_v[...] = scale
+    last = pltpu.make_async_copy(scale_v, scale_out, out_sem.at[4])
     last.start()
     for copy in first + second:
         copy.wait_send()
@@ -406,6 +422,25 @@
         copy.wait()
 
 
+def finish(left, right, moment, precond, scale, left_out, right_out, moment_out, update_out, held, sem):
+    load = pltpu.make_async_copy(precond.at[0], held, sem.at[4])
+    load.start()
+    moves = [
+        pltpu.make_async_copy(src, dst, sem.at[n])
+        for n, (src, dst) in enumerate(((left, left_out), (right, right_out), (moment, moment_out)))
+    ]
+    for move in moves:
+        move.start()
+    load.wait()
+    rows, order = held.shape[1:]
+    for s in range(SIDE):
+        held[s] = held[s] * jnp.broadcast_to(scale[s : s + 1, 0:1], (rows, order))
+    last = pltpu.make_async_copy(held, update_out.at[0], sem.at[3])
+    last.start()
+    for move in moves + [last]:
+        move.wait()
+
+
 def on_device(
     grads, left_stats, right_stats, left_root, right_root, second_moment, slot_block, counts
 ):
@@ -415,21 +450,19 @@
     slots, rows, order = left_stats.shape[1:]
     quads = blocks // SIDE
     stack = slots * rows
-    blocks = blocks
     hbm = pl.BlockSpec(memory_space=pl.ANY)
     smem = pl.BlockSpec(memory_space=pltpu.SMEM)
     out = jax.ShapeDtypeStruct(left_stats.shape, F32)
     dma = pltpu.SemaphoreType.DMA
     vmem = pltpu.VMEM
     n_dp = SIDE * SIDE
-    import functools
-
-    return tuple(
-        pl.pallas_call(
-            functools.partial(kernel, n_fsdp),
-            out_shape=(out,) * 4,
-            in_specs=[smem, smem] + [hbm] * 6,
-            out_specs=(hbm,) * 4,
+    small = [pltpu.with_memory_space_constraint(a, pltpu.HBM) for a in (slot_block.T, counts)]
+    pinned = [pltpu.with_memory_space_constraint(a, pltpu.HBM) for a in (grads, left_stats, right_stats, left_root, right_root, second_moment)]
+    results = pl.pallas_call(
+            functools.partial(kernel, n_fsdp, SPAN),
+            out_shape=(out,) * 4 + (jax.ShapeDtypeStruct((SIDE, LANES), F32),),
+            in_specs=[smem, smem] + [pl.BlockSpec(memory_space=pltpu.HBM)] * 6,
+            out_specs=(hbm,) * 5,
             scratch_shapes=[
                 vmem((blocks, slab, LANES), BF16),
                 vmem((SIDE - 1, blocks, slab, LANES), BF16),
@@ -450,22 +483,23 @@
                 vmem((slots, rows, order), F32),
                 vmem((slots, rows, order), F32),
                 vmem((slots, rows, order), F32),
-                vmem((2 * stack, order), BF16),
+                vmem((stack, order), BF16),
                 vmem((SIDE, stack, LANES), BF16),
                 vmem((SIDE, stack, LANES), F32),
                 vmem((SIDE, stack, LANES), F32),
                 vmem((8, LANES), F32),
                 vmem((n_dp - 1, 8, LANES), F32),
+                vmem((SIDE, LANES), F32),
                 dma((6,)),
-                dma((4,)),
+                dma((5,)),
                 dma((SIDE - 1,)),
                 dma((SIDE - 1,)),
                 dma((SIDE - 1,)),
                 dma((SIDE - 1,)),
                 dma,
-                dma((n_z // ZONE,)),
+                dma((n_z // SPAN,)),
                 dma,
-                dma((n_z // ZONE, 2, SIDE - 1)),
+                dma((n_z // SPAN, 2, SIDE - 1)),
                 dma,
                 dma,
                 dma,
@@ -473,10 +507,20 @@
                 pltpu.SemaphoreType.REGULAR((4,)),
             ],
             compiler_params=pltpu.CompilerParams(
-                collective_id=0, has_side_effects=True, vmem_limit_bytes=67043328
+                collective_id=0, has_side_effects=True, vmem_limit_bytes=24 << 20
             ),
             name="shampoo",
-        )(slot_block, counts, grads, left_stats, right_stats, left_root, right_root, second_moment)
+        )(*small, *pinned)
+    return tuple(
+        pl.pallas_call(
+            finish,
+            out_shape=(out,) * 4,
+            in_specs=[hbm] * 4 + [pl.BlockSpec(memory_space=pltpu.VMEM)],
+            out_specs=(hbm,) * 4,
+            scratch_shapes=[vmem((slots, rows, order), F32), dma((2 * 4,))],
+            compiler_params=pltpu.CompilerParams(vmem_limit_bytes=4 << 20),
+            name="finish",
+        )(*results)
     )
 
 

time: 87.3 us -> 73.7 us (0.84)
  local copies, waits for them, and re-layouts: 8.07 us -> 0 us
  Pallas kernels: 78.1 us -> 71.8 us
    unnamed x5 -> x0, local copies, waits for them, and re-layouts: 8.07 us -> none
    pallas_call x1 -> x2, Pallas kernels: 78.1 us -> 71.8 us  [the longest x1 70.7 us: on_device(): pl.pallas_call(functools.partial(kernel, n_fsdp, SPAN), out_shape=(out,)...]
where the time goes in v3:
time: 73.7 us; the launch traced here: 72.4 us
  Pallas kernels  71.8 us (97%)
    pallas_call x1, Pallas kernels, on_device(): pl.pallas_call(functools.partial(kernel, n_fsdp, SPAN), out_shape=(out,)...  70.7 us

profile of v3, /device:TPU:1, one launch (start us, length us, event | category | flops | bytes accessed | tf_op | source)
XLA Modules:
  0.0 72.4 jit_solution(6575716557196216665)
XLA Ops:
  0.6 70.7 %shampoo.1 = (f32[1,4,32,512]{3,2,1,0:T(8,128)S(1)}, f32[1,4,32,512]{3,2,1,0:T(8,128)S(1)}, f32[1,4,32,512]{3,2,1,0:T(8,128)S(1)}, f32[1,4,32,512]{3,2,1,0:T(8,128)S(1)}, f32[4,128]{1,0:T(4,128)S(1)}) custom-call(s32[4,64]{1,0:T(4,128)} %bitcast.1, s32[64]{0:T(128)} %count_ref.1, bf16[1,128,8,512]{3,2,1,0:T(8,128)(2,1)} %grads.1, ...), custom_call_target="tpu_custom_call" | custom-call | tf_op jit(solution)/shard_map/shampoo/pallas_call | solution.py:461
  71.4 1.1 %finish.1 = (f32[1,4,32,512]{3,2,1,0:T(8,128)}, f32[1,4,32,512]{3,2,1,0:T(8,128)}, f32[1,4,32,512]{3,2,1,0:T(8,128)}, f32[1,4,32,512]{3,2,1,0:T(8,128)}) custom-call(f32[1,4,32,512]{3,2,1,0:T(8,128)S(1)} %get-tuple-element.9.left, f32[1,4,32,512]{3,2,1,0:T(8,128)S(1)} %get-tuple-element.10.right, f32[1,4,32,512]{3,2,1,0:T(8,128)S(1)} %get-tuple-element.11.moment, ...), custom_call_target="tpu_custom_call" | custom-call | tf_op jit(solution)/shard_map/finish/pallas_call | solution.py:515

commit v4 on v3

--- a/solution.py
+++ b/solution.py
@@ -13,6 +13,7 @@
 
 SIDE = 4
 LANES = 128
+CHUNKS = 2
 SPAN = 4
 PART = LANES // SIDE
 F32 = jnp.float32
@@ -112,7 +113,7 @@
         )
 
     own_load = pltpu.make_async_copy(
-        grads.at[0, :, :, pl.ds(pl.multiple_of(i1 * LANES, LANES), LANES)], own_tile, load_sem.at[0]
+        grads.at[0, :, :, :, pl.ds(pl.multiple_of(i1 * LANES, LANES), LANES)], own_tile, load_sem.at[0]
     )
     own_load.start()
 
@@ -134,18 +135,21 @@
         load.start()
     pl.semaphore_wait(barrier, len(greeted))
 
+    quads, slab = own_tile.shape[1:3]
+    count = quads // CHUNKS
     first = []
-    for k in (2, 1, 3):
-        tile = pl.ds(pl.multiple_of(((i1 + k) % SIDE) * LANES, LANES), LANES)
-        copy = remote(
-            grads.at[0, :, :, tile],
-            first_in.at[k - 1],
-            first_send_sem.at[k - 1],
-            first_recv_sem.at[k - 1],
-            first_peer(k),
-        )
-        copy.start()
-        first.append(copy)
+    for ch in range(CHUNKS):
+        for k in (2, 1, 3):
+            tile = pl.ds(pl.multiple_of(((i1 + k) % SIDE) * LANES, LANES), LANES)
+            copy = remote(
+                grads.at[0, :, pl.ds(ch * count, count), :, tile],
+                first_in.at[k - 1, :, pl.ds(ch * count, count)],
+                first_send_sem.at[ch, k - 1],
+                first_recv_sem.at[ch, k - 1],
+                first_peer(k),
+            )
+            copy.start()
+            first.append(copy)
 
     row = lax.broadcasted_iota(jnp.int32, (SIDE * LANES, SIDE * LANES), 0)
     col = lax.broadcasted_iota(jnp.int32, (SIDE * LANES, SIDE * LANES), 1)
@@ -174,36 +178,42 @@
         tell(n)
 
     own_load.wait()
-    for copy in first:
-        copy.wait_recv()
-    quads = own_tile.shape[0] // SIDE
-    for i in range(SIDE):
-        total = own_tile[i * quads : (i + 1) * quads].astype(F32)
+    second = []
+    for ch in range(CHUNKS):
+        for copy in first[ch * (SIDE - 1) : (ch + 1) * (SIDE - 1)]:
+            copy.wait_recv()
+        some = slice(ch * count, (ch + 1) * count)
+        lines = slice(ch * count * slab, (ch + 1) * count * slab)
+        for i in range(SIDE):
+            total = own_tile[i, some].astype(F32)
+            for k in range(SIDE - 1):
+                total += first_in[k, i, some].astype(F32)
+            stacked[lines, i * LANES : (i + 1) * LANES] = total.reshape(count * slab, LANES).astype(BF16)
+        packed = jnp.dot(stacked[lines, :], perm[...], preferred_element_type=F32)
+        for q in range(SIDE):
+            second_send[q, lines] = packed[:, q * LANES : (q + 1) * LANES].astype(BF16)
+        for k in (2, 1, 3):
+            copy = remote(
+                second_send.at[(i2 + k) % SIDE, pl.ds(ch * count * slab, count * slab)],
+                second_in.at[k - 1, pl.ds(ch * count * slab, count * slab)],
+                second_send_sem.at[ch, k - 1],
+                second_recv_sem.at[ch, k - 1],
+                second_peer(k),
+            )
+            copy.start()
+            second.append(copy)
+    for ch in range(CHUNKS):
+        for copy in second[ch * (SIDE - 1) : (ch + 1) * (SIDE - 1)]:
+            copy.wait_recv()
+        lines = slice(ch * count * slab, (ch + 1) * count * slab)
+        total = second_send[i2, lines].astype(F32)
         for k in range(SIDE - 1):
-            total += first_in[k, i * quads : (i + 1) * quads].astype(F32)
-        stacked[:, i * LANES : (i + 1) * LANES] = total.reshape(quads * 8, LANES).astype(BF16)
-    packed = jnp.dot(stacked[...], perm[...], preferred_element_type=F32)
-    for q in range(SIDE):
-        second_send[q] = packed[:, q * LANES : (q + 1) * LANES].astype(BF16)
-    second = []
-    for k in (2, 1, 3):
-        copy = remote(
-            second_send.at[(i2 + k) % SIDE],
-            second_in.at[k - 1],
-            second_send_sem.at[k - 1],
-            second_recv_sem.at[k - 1],
-            second_peer(k),
-        )
-        copy.start()
-        second.append(copy)
-    total = second_send[i2].astype(F32)
-    for copy in second:
-        copy.wait_recv()
-    for k in range(SIDE - 1):
-        total += second_in[k].astype(F32)
-    spread = jnp.dot(total.astype(BF16), rep[...], preferred_element_type=F32)
-    for i in range(SIDE):
-        table[i * quads : (i + 1) * quads] = spread[:, i * LANES : (i + 1) * LANES].reshape(quads, 8, LANES)
+            total += second_in[k, lines].astype(F32)
+        spread = jnp.dot(total.astype(BF16), rep[...], preferred_element_type=F32)
+        for i in range(SIDE):
+            table[i * quads + ch * count : i * quads + (ch + 1) * count] = spread[
+                :, i * LANES : (i + 1) * LANES
+            ].reshape(count, slab, LANES)
 
     lane = lax.broadcasted_iota(jnp.int32, (8, LANES), 1) // PART
 
@@ -457,15 +467,15 @@
     vmem = pltpu.VMEM
     n_dp = SIDE * SIDE
     small = [pltpu.with_memory_space_constraint(a, pltpu.HBM) for a in (slot_block.T, counts)]
-    pinned = [pltpu.with_memory_space_constraint(a, pltpu.HBM) for a in (grads, left_stats, right_stats, left_root, right_root, second_moment)]
+    pinned = [pltpu.with_memory_space_constraint(a, pltpu.HBM) for a in (grads.reshape(1, SIDE, quads, slab, order), left_stats, right_stats, left_root, right_root, second_moment)]
     results = pl.pallas_call(
             functools.partial(kernel, n_fsdp, SPAN),
             out_shape=(out,) * 4 + (jax.ShapeDtypeStruct((SIDE, LANES), F32),),
             in_specs=[smem, smem] + [pl.BlockSpec(memory_space=pltpu.HBM)] * 6,
             out_specs=(hbm,) * 5,
             scratch_shapes=[
-                vmem((blocks, slab, LANES), BF16),
-                vmem((SIDE - 1, blocks, slab, LANES), BF16),
+                vmem((SIDE, quads, slab, LANES), BF16),
+                vmem((SIDE - 1, SIDE, quads, slab, LANES), BF16),
                 vmem((quads * slab, SIDE * LANES), BF16),
                 vmem((SIDE * LANES, SIDE * LANES), BF16),
                 vmem((LANES, SIDE * LANES), BF16),
@@ -492,10 +502,10 @@
                 vmem((SIDE, LANES), F32),
                 dma((6,)),
                 dma((5,)),
-                dma((SIDE - 1,)),
-                dma((SIDE - 1,)),
-                dma((SIDE - 1,)),
-                dma((SIDE - 1,)),
+                dma((CHUNKS, SIDE - 1)),
+                dma((CHUNKS, SIDE - 1)),
+                dma((CHUNKS, SIDE - 1)),
+                dma((CHUNKS, SIDE - 1)),
                 dma,
                 dma((n_z // SPAN,)),
                 dma,

time: 73.7 us -> 72.6 us (0.985)
  Pallas kernels: 71.8 us -> 70.7 us
    pallas_call x1, Pallas kernels: 70.7 us -> 69.7 us  [on_device(): pl.pallas_call(functools.partial(kernel, n_fsdp, SPAN), out_shape=(out,)...]
where the time goes in v4:
time: 72.6 us; the launch traced here: 71.4 us
  Pallas kernels  70.7 us (97%)
    pallas_call x1, Pallas kernels, on_device(): pl.pallas_call(functools.partial(kernel, n_fsdp, SPAN), out_shape=(out,)...  69.7 us

profile of v4, /device:TPU:1, one launch (start us, length us, event | category | flops | bytes accessed | tf_op | source)
XLA Modules:
  0.0 71.4 jit_solution(9308917317891539896)
XLA Ops:
  0.6 69.7 %shampoo.1 = (f32[1,4,32,512]{3,2,1,0:T(8,128)S(1)}, f32[1,4,32,512]{3,2,1,0:T(8,128)S(1)}, f32[1,4,32,512]{3,2,1,0:T(8,128)S(1)}, f32[1,4,32,512]{3,2,1,0:T(8,128)S(1)}, f32[4,128]{1,0:T(4,128)S(1)}) custom-call(s32[4,64]{1,0:T(4,128)} %bitcast.3, s32[64]{0:T(128)} %count_ref.1, bf16[1,4,32,8,512]{4,3,2,1,0:T(8,128)(2,1)} %bitcast.2, ...), custom_call_target="tpu_custom_call" | custom-call | tf_op jit(solution)/shard_map/shampoo/pallas_call | solution.py:471
  70.3 1.1 %finish.1 = (f32[1,4,32,512]{3,2,1,0:T(8,128)}, f32[1,4,32,512]{3,2,1,0:T(8,128)}, f32[1,4,32,512]{3,2,1,0:T(8,128)}, f32[1,4,32,512]{3,2,1,0:T(8,128)}) custom-call(f32[1,4,32,512]{3,2,1,0:T(8,128)S(1)} %get-tuple-element.9.left, f32[1,4,32,512]{3,2,1,0:T(8,128)S(1)} %get-tuple-element.10.right, f32[1,4,32,512]{3,2,1,0:T(8,128)S(1)} %get-tuple-element.11.moment, ...), custom_call_target="tpu_custom_call" | custom-call | tf_op jit(solution)/shard_map/finish/pallas_call | solution.py:525

commit v5 on v4

--- a/solution.py
+++ b/solution.py
@@ -13,7 +13,7 @@
 
 SIDE = 4
 LANES = 128
-CHUNKS = 2
+CHUNKS = 4
 SPAN = 4
 PART = LANES // SIDE
 F32 = jnp.float32
@@ -228,7 +228,6 @@
 
     lax.fori_loop(0, n_fsdp, pick, 0, unroll=4)
 
-    pl.semaphore_wait(met.at[len(reach) - 1], 2)
     mine = i1 * SIDE + i2
     zone = z // span
     keep = pltpu.make_async_copy(message.at[owner], gathered.at[mine, z, core], swap_recv_sem.at[zone])
@@ -247,7 +246,9 @@
                 send_to(((z + step) % n_z) * 2 + c)
         return carry
 
-    lax.fori_loop(0, n_z // 2 - 1, swap, 0, unroll=5)
+    lax.fori_loop(0, reach[-1], swap, 0, unroll=4)
+    pl.semaphore_wait(met.at[len(reach) - 1], 2)
+    lax.fori_loop(reach[-1], n_z // 2 - 1, swap, 0, unroll=7)
     for c in range(2):
         send_to(((z + n_z // 2) % n_z) * 2 + c)
 
@@ -380,12 +381,11 @@
 
     n_dp = SIDE * SIDE
 
-    def share(n, carry):
-        to = ((dp + n + 1) % n_dp, owner)
+    steps = [(kx, ky) for kx in range(SIDE) for ky in range(SIDE) if kx or ky]
+    steps.sort(key=lambda k: -sum(min(n, SIDE - n) for n in k))
+    for n, (kx, ky) in enumerate(steps):
+        to = (((gx + kx) % SIDE) * SIDE + (gy + ky) % SIDE, owner)
         remote(norm_out, norm_in.at[n], norm_send_sem, norm_recv_sem, to).start()
-        return carry
-
-    lax.fori_loop(0, n_dp - 1, share, 0)
     lhs_v[...] = piece(dp).T
     left_sum = lax.fori_loop(0, SIDE, terms, jnp.zeros((stack, order), F32))
     for s in range(SIDE):

time: 72.6 us -> 72.9 us (level)
  no operation moved by 1% of the time
where the time goes in v5:
time: 72.9 us; the launch traced here: 71.4 us
  Pallas kernels  70.8 us (97%)
    pallas_call x1, Pallas kernels, on_device(): pl.pallas_call(functools.partial(kernel, n_fsdp, SPAN), out_shape=(out,)...  69.7 us

profile of v5, /device:TPU:1, one launch (start us, length us, event | category | flops | bytes accessed | tf_op | source)
XLA Modules:
  0.0 71.4 jit_solution(8342299403653283734)
XLA Ops:
  0.6 69.7 %shampoo.1 = (f32[1,4,32,512]{3,2,1,0:T(8,128)S(1)}, f32[1,4,32,512]{3,2,1,0:T(8,128)S(1)}, f32[1,4,32,512]{3,2,1,0:T(8,128)S(1)}, f32[1,4,32,512]{3,2,1,0:T(8,128)S(1)}, f32[4,128]{1,0:T(4,128)S(1)}) custom-call(s32[4,64]{1,0:T(4,128)} %bitcast.3, s32[64]{0:T(128)} %count_ref.1, bf16[1,4,32,8,512]{4,3,2,1,0:T(8,128)(2,1)} %bitcast.2, ...), custom_call_target="tpu_custom_call" | custom-call | tf_op jit(solution)/shard_map/shampoo/pallas_call | solution.py:471
  70.3 1.1 %finish.1 = (f32[1,4,32,512]{3,2,1,0:T(8,128)}, f32[1,4,32,512]{3,2,1,0:T(8,128)}, f32[1,4,32,512]{3,2,1,0:T(8,128)}, f32[1,4,32,512]{3,2,1,0:T(8,128)}) custom-call(f32[1,4,32,512]{3,2,1,0:T(8,128)S(1)} %get-tuple-element.9.left, f32[1,4,32,512]{3,2,1,0:T(8,128)S(1)} %get-tuple-element.10.right, f32[1,4,32,512]{3,2,1,0:T(8,128)S(1)} %get-tuple-element.11.moment, ...), custom_call_target="tpu_custom_call" | custom-call | tf_op jit(solution)/shard_map/finish/pallas_call | solution.py:525
